TPU v7x, 32 devices: a whole 2x2x4 slice. The times are simulated.
32 devices in a mesh: box: 4 (over z), row: 4 (over y, core), col: 2 (over x).
Axes of the slice: x: 2, y: 2, z: 4, core: 2. Of those that a mesh axis runs over, the one named last changes fastest.
Arguments:
- ext_ext: float32 [4, 3072, 3072], P('box', 'row', 'col'), may hold values from -6 to 6
- ext_int: float32 [4, 3072, 1024], P('box', 'row', 'col'), may hold values from -0.1875 to 0.1875
- int_ext: float32 [4, 1024, 3072], P('box', 'row', 'col'), may hold values from -6 to 6
- int_int: float32 [4, 1024, 1024], P('box', 'row', 'col'), may hold values from -0.1 to 0.1, as said below
Outputs:
- merged: float32 [4, 3072, 2, 3072], P('box', 'row', None, 'col')
Inputs may be any that keep to these rules, and one draw needn't show every extreme that they name: `int_int`: independent entries.
All inputs are finite; a program needn't handle non-finite values.
Results may differ from a plain program's by a relative error of at most 0.0003.
Values sent between devices are 32-bit elements; how exact they have to be, the bound alone decides.
No kernel may reach another device: no remote copies, remote signals or barrier semaphores. Data moves between devices by JAX's collectives and lax.ppermute only.
A program may use at most 128 MiB of HBM per device.

v0:
```python
import jax
import jax.numpy as jnp
from jax import lax
from jax.sharding import PartitionSpec as P

HIGH = lax.Precision.HIGHEST


def swapped(shard, axis, distance):
    return lax.ppermute(shard, axis, [(i, i ^ 1 << distance) for i in range(lax.axis_size(axis))])


def panel_dot(total, piece, panel):
    return total + jnp.dot(piece, panel, precision=HIGH, preferred_element_type=jnp.float32)


def chain_product(left, right):
    panel = lax.all_gather(right, "row", axis=0, tiled=True)
    empty = jnp.zeros((left.shape[0], right.shape[1]), jnp.float32)
    return panel_dot(empty, lax.all_gather(left, "col", axis=1, tiled=True), panel)


def local(ext_ext, ext_int, int_ext, int_int):
    own_ee = ext_ext[0]
    own_ed = ext_int[0]
    own_de = int_ext[0]
    own_dd = int_int[0]
    partner_dd, partner_de = swapped((own_dd, own_de), "box", 0)
    is_even = lax.axis_index("box") % 2 == 0
    block_rows = own_dd.shape[0]
    block_cols = own_dd.shape[1]
    row_ids = lax.axis_index("row") * block_rows + lax.broadcasted_iota(
        jnp.int32, (block_rows, block_cols), 0
    )
    col_ids = lax.axis_index("col") * block_cols + lax.broadcasted_iota(
        jnp.int32, (block_rows, block_cols), 1
    )
    identity = (row_ids == col_ids).astype(jnp.float32)
    coupling = chain_product(partner_dd, own_dd)
    square = chain_product(coupling, coupling)
    first = identity + coupling
    inverse = first + chain_product(first, square)
    de_panel = lax.all_gather(own_de, "row", axis=0, tiled=True)
    coupled = panel_dot(
        jnp.zeros(own_de.shape, jnp.float32),
        lax.all_gather(partner_dd, "col", axis=1, tiled=True),
        de_panel,
    )
    source = jnp.concatenate(
        [jnp.where(is_even, coupled, partner_de), jnp.where(is_even, partner_de, coupled)], axis=1
    )
    source_panel = lax.all_gather(source, "row", axis=0, tiled=True)
    pieces = lax.all_gather(inverse[None], ("row", "col"), axis=0, tiled=True)
    row_count = lax.axis_size("row")
    col_count = lax.axis_size("col")
    whole = pieces.reshape(row_count, col_count, block_rows, block_cols).transpose(0, 2, 1, 3)
    whole = whole.reshape(row_count * block_rows, col_count * block_cols)
    right_panel = jnp.dot(whole, source_panel, precision=HIGH, preferred_element_type=jnp.float32)
    zeros = jnp.zeros_like(own_ee)
    start_terms = jnp.concatenate(
        [jnp.where(is_even, own_ee, zeros), jnp.where(is_even, zeros, own_ee)], axis=1
    )
    merged = panel_dot(start_terms, lax.all_gather(own_ed, "col", axis=1, tiled=True), right_panel)
    return merged.reshape(1, own_ee.shape[0], 2, own_ee.shape[1])


def solution(mesh):
    placed = (
        P("box", "row", "col"),
        P("box", "row", "col"),
        P("box", "row", "col"),
        P("box", "row", "col"),
    )
    return jax.shard_map(
        local, mesh=mesh, in_specs=placed, out_specs=P("box", "row", None, "col"), check_vma=False
    )
```

profile of v0, /device:TPU:0, one launch (start us, length us, event | category | flops | bytes accessed | tf_op | source)
XLA Modules:
  0.0 469.0 jit_solution(2206762846612566274)
XLA Ops:
  6.5 3.1 collective-permute-start
  9.6 12.1 %collective-permute-done = f32[256,512]{1,0:T(8,128)S(1)} collective-permute-done((f32[256,512]{1,0:T(8,128)}, f32[256,512]{1,0:T(8,128)S(1)}, u32[]{:S(2)}, u32[]{:S(2)}) %collective-permute-start) | collective-permute-done | bytes 524320 | tf_op jit(solution)/shard_map/ppermute | solution.py:10
  23.4 22.0 %all-gather.15.cloned.1.call-done = f32[256,1024]{1,0:T(8,128)} async-done(((f32[256,512]{1,0:T(8,128)}), f32[256,1024]{1,0:T(8,128)}) %all-gather.15.cloned.1.call-update) | async-done | bytes 1048592 | tf_op jit(solution)/shard_map/all_gather | solution.py:20
  45.4 24.2 %all-gather.27.cloned.1.call-done = f32[1,1024,512]{2,1,0:T(8,128)} async-done(((f32[1,256,512]{2,1,0:T(8,128)}), f32[1,1024,512]{2,1,0:T(8,128)}) %all-gather.27.cloned.1.call-update) | async-done | bytes 2097168 | tf_op jit(solution)/shard_map/all_gather | solution.py:18
  69.5 4.8 %convert_add_fusion = (f32[256,512]{1,0:T(8,128)}, f32[256,512]{1,0:T(8,128)}) fusion(s32[512]{0:T(512)S(1)} %iota_add_fusion, s32[256]{0:T(256)S(1)} %iota_add_fusion.1, f32[256,1024]{1,0:T(8,128)} %all-gather.15.cloned.1.call-done, f32[1,1024,512]{2,1,0:T(8,128)} %all-gather.27.cloned.1.call-done), kind=kOutput, calls=%fused_computation.12 | convolution fusion | flops 1611005952 | bytes 4197376 | tf_op jit(solution)/shard_map/dot_general | solution.py:14
  75.6 20.2 %all-gather.19.cloned.1.call-done = f32[256,1024]{1,0:T(8,128)} async-done(((f32[256,512]{1,0:T(8,128)}), f32[256,1024]{1,0:T(8,128)}) %all-gather.19.cloned.1.call-update) | async-done | bytes 1048592 | tf_op jit(solution)/shard_map/all_gather | solution.py:20
  95.8 24.0 %all-gather.21.cloned.1.call-done = f32[1024,512]{1,0:T(8,128)} async-done(((f32[256,512]{1,0:T(8,128)}), f32[1024,512]{1,0:T(8,128)}) %all-gather.21.cloned.1.call-update) | async-done | bytes 2097168 | tf_op jit(solution)/shard_map/all_gather | solution.py:18
  119.8 4.6 fusion.5
  125.3 17.2 %all-gather.17.cloned.1.call-done = f32[256,1024]{1,0:T(8,128)} async-done(((f32[256,512]{1,0:T(8,128)}), f32[256,1024]{1,0:T(8,128)}) %all-gather.17.cloned.1.call-update) | async-done | bytes 1048592 | tf_op jit(solution)/shard_map/all_gather | solution.py:20
  142.5 24.0 %all-gather.23.cloned.1.call-done = f32[1024,512]{1,0:T(8,128)} async-done(((f32[256,512]{1,0:T(8,128)}), f32[1024,512]{1,0:T(8,128)}) %all-gather.23.cloned.1.call-update) | async-done | bytes 2097168 | tf_op jit(solution)/shard_map/all_gather | solution.py:18
  166.6 4.6 convolution_add_fusion
  172.8 35.3 %collective-permute-done.1 = f32[256,1536]{1,0:T(8,128)S(1)} collective-permute-done((f32[256,1536]{1,0:T(8,128)}, f32[256,1536]{1,0:T(8,128)S(1)}, u32[]{:S(2)}, u32[]{:S(2)}) %collective-permute-start.1) | collective-permute-done | bytes 1572896 | tf_op jit(solution)/shard_map/ppermute | solution.py:10
  208.1 6.4 %all-gather.31.cloned.1.call-done = f32[1,1024,1536]{2,1,0:T(8,128)} async-done(((f32[1,256,1536]{2,1,0:T(8,128)}), f32[1,1024,1536]{2,1,0:T(8,128)}) %all-gather.31.cloned.1.call-update) | async-done | bytes 6291472 | tf_op jit(solution)/shard_map/all_gather | solution.py:43
  214.5 7.6 %broadcast_select_fusion.1 = (f32[256,1536]{1,0:T(8,128)S(1)}, f32[256,1536]{1,0:T(8,128)S(1)}) fusion(f32[256,1536]{1,0:T(8,128)S(1)} %collective-permute-done.1, pred[]{:T(512)S(6)} %eq.8, f32[256,1024]{1,0:T(8,128)S(1)} %copy-done.1, f32[1,1024,1536]{2,1,0:T(8,128)} %all-gather.31.cloned.1.call-done), kind=kOutput, calls=%fused_computation.11 | convolution fusion | flops 4832624640 | bytes 12058625 | tf_op jit(solution)/shard_map/dot_general | solution.py:14
  222.1 1.9 pad_maximum_fusion
  224.7 6.1 %copy.8 = f32[1,768,1536]{1,2,0:T(8,128)} copy(f32[1,768,1536]{2,1,0:T(8,128)} %param.4) | data formatting | bytes 9437184 | tf_op args[0]
  230.7 6.7 %select_bitcast_fusion.1 = (f32[768,1536]{0,1:T(8,128)}, f32[768,1536]{0,1:T(8,128)}) fusion(f32[1,768,1536]{1,2,0:T(8,128)} %copy.8, pred[]{:T(512)S(6)} %eq.8), kind=kLoop, calls=%fused_computation.4 | loop fusion | flops 2359296 | bytes 14155777 | tf_op jit(solution)/shard_map/jit(_where)/select_n | solution.py:61
  237.4 15.6 %all-gather.29.cloned.1.call-done = f32[2048,512]{1,0:T(8,128)} async-done(((f32[256,512]{1,0:T(8,128)}), f32[2048,512]{1,0:T(8,128)}) %all-gather.29.cloned.1.call-update) | async-done | bytes 4194320 | tf_op jit(solution)/shard_map/all_gather | solution.py:53
  253.0 5.4 %copy.10 = f32[4,2,256,512]{3,1,2,0:T(2,128)S(1)} copy(f32[4,2,256,512]{3,2,1,0:T(8,128)} %bitcast.38) | data formatting | bytes 8388608 | tf_op jit(solution)/shard_map/reshape | solution.py:56
  258.4 3.1 copy.12
  261.5 75.2 %all-gather.25.cloned.1.call-done = f32[1024,3072]{1,0:T(8,128)} async-done(((f32[256,3072]{1,0:T(8,128)}), f32[1024,3072]{1,0:T(8,128)}) %all-gather.25.cloned.1.call-update) | async-done | bytes 12582928 | tf_op jit(solution)/shard_map/all_gather | solution.py:52
  336.7 44.8 %fusion.6 = f32[1024,3072]{1,0:T(8,128)} fusion(f32[1024,1024]{1,0:T(8,128)} %bitcast.39, f32[1024,3072]{1,0:T(8,128)} %all-gather.25.cloned.1.call-done), kind=kOutput, calls=%fused_computation.16 | convolution fusion | flops 38654705664 | bytes 29360128 | tf_op jit(solution)/shard_map/dot_general | solution.py:58
  383.0 64.4 %maximum_add_fusion = f32[768,3072]{0,1:T(8,128)} fusion(f32[768,1536]{0,1:T(8,128)} %get-tuple-element.6, f32[768,1536]{0,1:T(8,128)} %get-tuple-element.5, f32[1024,3072]{1,0:T(8,128)} %fusion.6, f32[1,768,1024]{2,1,0:T(8,128)} %all-gather.33.cloned.1.call-done), kind=kOutput, calls=%fused_computation | convolution fusion | flops 28995747840 | bytes 34603008 | tf_op jit(solution)/shard_map/dot_general | solution.py:14
  447.4 14.8 %copy.11 = f32[1,768,2,1536]{3,2,1,0:T(2,128)} copy(f32[1,768,2,1536]{1,3,2,0:T(8,128)} %bitcast.37) | data formatting | bytes 18874368 | tf_op jit(solution)/shard_map/reshape | solution.py:64
  (30 shorter events, 7.3 us)
Async XLA Ops:
  6.5 38.9 %all-gather.15.cloned.1.call-start = ((), (), s32[]{:S(2)}) async-start(), calls=%async_computation | async-start | bytes 1572864 | tf_op jit(solution)/shard_map/all_gather | solution.py:20
  6.5 15.2 %collective-permute-start = (f32[256,512]{1,0:T(8,128)}, f32[256,512]{1,0:T(8,128)S(1)}, u32[]{:S(2)}, u32[]{:S(2)}) collective-permute-start(f32[256,512]{1,0:T(8,128)} %bitcast.41), channel_id=1, source_target_pairs={{0,8},{8,0},{16,24},{24,16},{1,9},{9,1},{17,25},{25,17},{2,10},{10... | collective-permute-start | bytes 1572872 | tf_op jit(solution)/shard_map/ppermute | solution.py:10
  21.7 0.8 copy-start.2
  22.5 47.0 %all-gather.27.cloned.1.call-start = ((), (), s32[]{:S(2)}) async-start(), calls=%async_computation.6 | async-start | bytes 2621440 | tf_op jit(solution)/shard_map/all_gather | solution.py:18
  23.3 72.5 %all-gather.19.cloned.1.call-start = ((), (), s32[]{:S(2)}) async-start(), calls=%async_computation.2 | async-start | bytes 1572864 | tf_op jit(solution)/shard_map/all_gather | solution.py:20
  74.4 92.2 %copy-start = (f32[256,512]{1,0:T(8,128)S(1)}, f32[256,512]{1,0:T(8,128)}, u32[]{:S(2)}) copy-start(f32[256,512]{1,0:T(8,128)} %get-tuple-element.9) | copy-start | bytes 1572868
  74.4 45.4 %all-gather.21.cloned.1.call-start = ((), (), s32[]{:S(2)}) async-start(), calls=%async_computation.3 | async-start | bytes 2621440 | tf_op jit(solution)/shard_map/all_gather | solution.py:18
  75.0 67.6 %all-gather.17.cloned.1.call-start = ((), (), s32[]{:S(2)}) async-start(), calls=%async_computation.1 | async-start | bytes 1572864 | tf_op jit(solution)/shard_map/all_gather | solution.py:20
  75.6 91.0 %all-gather.23.cloned.1.call-start = ((), (), s32[]{:S(2)}) async-start(), calls=%async_computation.4 | async-start | bytes 2621440 | tf_op jit(solution)/shard_map/all_gather | solution.py:18
  124.5 90.0 %copy-start.1 = (f32[256,1024]{1,0:T(8,128)S(1)}, f32[256,1024]{1,0:T(8,128)}, u32[]{:S(2)}) copy-start(f32[256,1024]{1,0:T(8,128)} %all-gather.15.cloned.1.call-done) | copy-start | bytes 3145732
  124.5 90.0 %all-gather.31.cloned.1.call-start = ((), (), s32[]{:S(2)}) async-start(), calls=%async_computation.8 | async-start | bytes 7864320 | tf_op jit(solution)/shard_map/all_gather | solution.py:43
  125.3 127.7 %all-gather.29.cloned.1.call-start = ((), (), s32[]{:S(2)}) async-start(), calls=%async_computation.7 | async-start | bytes 4718592 | tf_op jit(solution)/shard_map/all_gather | solution.py:53
  171.2 165.5 %all-gather.25.cloned.1.call-start = ((), (), s32[]{:S(2)}) async-start(), calls=%async_computation.5 | async-start | bytes 15728640 | tf_op jit(solution)/shard_map/all_gather | solution.py:52
  171.3 36.8 %collective-permute-start.1 = (f32[256,1536]{1,0:T(8,128)}, f32[256,1536]{1,0:T(8,128)S(1)}, u32[]{:S(2)}, u32[]{:S(2)}) collective-permute-start(f32[256,1536]{1,0:T(8,128)} %bitcast.40), channel_id=1, source_target_pairs={{0,8},{8,0},{16,24},{24,16},{1,9},{9,1},{17,25},{25,17},{2,10},{10... | collective-permute-start | bytes 4718600 | tf_op jit(solution)/shard_map/ppermute | solution.py:10
  224.1 158.9 %all-gather.33.cloned.1.call-start = ((), (), s32[]{:S(2)}) async-start(), calls=%async_computation.9 | async-start | bytes 4718592 | tf_op jit(solution)/shard_map/all_gather | solution.py:63
Sparse Core Ops, SparseCore 0:
  22.7 22.6 all-gather.14
  46.9 22.5 all-gather.26
  74.5 21.2 all-gather.18
  97.2 22.5 all-gather.20
  121.2 21.2 all-gather.16
  143.9 22.5 all-gather.22
  168.1 46.3 all-gather.30
  216.4 36.5 all-gather.28
  254.6 82.0 all-gather.24
  338.1 44.8 all-gather.32
where the time goes:
time: 470 us; the launch traced here: 469 us
  waiting for transfers between devices  281 us (60%)
  matrix products  131 us (28%)
  local copies, waits for them, and re-layouts  30.1 us (6%)
  between operations  13.6 us (3%)
  other arithmetic  8.65 us (2%)
  starting transfers between devices  5.14 us (1%)
    dot_general x5, matrix products, panel_dot(): jnp.dot(piece, panel, precision=HIGH, preferred_element_type=jnp.float32)  86.1 us
    all_gather x1, waiting for transfers between devices, local(): source_panel = lax.all_gather(source, 'row', axis=0, tiled=True)  75.2 us
    all_gather x3, waiting for transfers between devices, chain_product(): panel = lax.all_gather(right, 'row', axis=0, tiled=True)  72.2 us
    all_gather x3, waiting for transfers between devices, chain_product(): lax.all_gather(left, 'col', axis=1, tiled=True)  59.5 us
    ppermute x2, waiting for transfers between devices, swapped(): lax.ppermute(shard, axis, [(i, i ^ 1 << distance) for i in range(lax.axis...  47.4 us
    dot_general x1, matrix products, local(): jnp.dot(whole, source_panel, precision=HIGH, preferred_element_type=jnp.f...  44.8 us
    all_gather x1, waiting for transfers between devices, local(): pieces = lax.all_gather(inverse[None], ('row', 'col'), axis=0, tiled=True)  15.6 us
    reshape x1, local copies, waits for them, and re-layouts, local(): return merged.reshape(1, own_ee.shape[0], 2, own_ee.shape[1])  14.8 us
  transfers between devices with their start and end apart: 12, of which 12 were waited for; matrix products, arithmetic and copies ran while one was open for 18% of the time, Pallas kernels for 0%

commit v1 on v0

--- a/solution.py
+++ b/solution.py
@@ -15,7 +15,19 @@
 
 
 def chain_product(left, right):
-    panel = lax.all_gather(right, "row", axis=0, tiled=True)
+
+    def unite_notes_for(packet, link_axis):
+        slots = lax.axis_size(link_axis)
+        frames = [packet]
+        for hop_no in range(slots - 1):
+            k_now = lax.ppermute(
+                frames[-1], link_axis, [(tick, (tick + 1) % slots) for tick in range(slots)]
+            )
+            frames.append(k_now)
+        before = jnp.concatenate(frames[::-1], 0)
+        return jnp.roll(before, (lax.axis_index(link_axis) + 1) * packet.shape[0], axis=0)
+
+    panel = unite_notes_for(right, "row")
     empty = jnp.zeros((left.shape[0], right.shape[1]), jnp.float32)
     return panel_dot(empty, lax.all_gather(left, "col", axis=1, tiled=True), panel)
 

time: 470 us -> 407 us (0.87); the launches traced: 469 us -> 399 us
  waiting for transfers between devices: 281 us -> 209 us
    all_gather x3 -> x0, waiting for transfers between devices: 72.2 us -> none  [chain_product(): panel = lax.all_gather(right, 'row', axis=0, tiled=True)]
    ppermute x0 -> x9, waiting for transfers between devices: none -> 60.6 us  [unite_notes_for(): lax.ppermute(frames[-1], link_axis, [(tick, (tick + 1) % slots) for tick...]
    all_gather x3, waiting for transfers between devices: 59.5 us -> 16.7 us  [chain_product(): lax.all_gather(left, 'col', axis=1, tiled=True)]
    all_gather x1, waiting for transfers between devices: 15.6 us -> 5.26 us  [local(): pieces = lax.all_gather(inverse[None], ('row', 'col'), axis=0, tiled=True)]
    all_gather x1, waiting for transfers between devices: 6.43 us -> 0.01 us  [local(): de_panel = lax.all_gather(own_de, 'row', axis=0, tiled=True)]
  transfers between devices with their start and end apart: 12 -> 18, of which waited for: 12 -> 14; matrix products, arithmetic and copies ran while one was open for 18% -> 21% of each run, Pallas kernels for 0% -> 0%
where the time goes in v1:
time: 407 us; the launch traced here: 399 us
  waiting for transfers between devices  209 us (51%)
  matrix products  132 us (32%)
  local copies, waits for them, and re-layouts  30.2 us (7%)
  between operations  14 us (3%)
  other arithmetic  8.67 us (2%)
  starting transfers between devices  5.14 us (1%)
    dot_general x5, matrix products, panel_dot(): jnp.dot(piece, panel, precision=HIGH, preferred_element_type=jnp.float32)  87.6 us
    all_gather x1, waiting for transfers between devices, local(): source_panel = lax.all_gather(source, 'row', axis=0, tiled=True)  75 us
    ppermute x9, waiting for transfers between devices, unite_notes_for(): lax.ppermute(frames[-1], link_axis, [(tick, (tick + 1) % slots) for tick...  60.6 us
    ppermute x2, waiting for transfers between devices, swapped(): lax.ppermute(shard, axis, [(i, i ^ 1 << distance) for i in range(lax.axis...  47.5 us
    dot_general x1, matrix products, local(): jnp.dot(whole, source_panel, precision=HIGH, preferred_element_type=jnp.f...  44.8 us
    all_gather x3, waiting for transfers between devices, chain_product(): lax.all_gather(left, 'col', axis=1, tiled=True)  16.7 us
    reshape x1, local copies, waits for them, and re-layouts, local(): return merged.reshape(1, own_ee.shape[0], 2, own_ee.shape[1])  14.8 us
    unnamed x8, local copies, waits for them, and re-layouts  10 us
  transfers between devices with their start and end apart: 18, of which 14 were waited for; matrix products, arithmetic and copies ran while one was open for 21% of the time, Pallas kernels for 0%

profile of v1, /device:TPU:0, one launch (start us, length us, event | category | flops | bytes accessed | tf_op | source)
XLA Modules:
  0.0 399.1 jit_solution(3581380616287302409)
XLA Ops:
  6.5 3.1 collective-permute-start.3
  9.6 12.1 %collective-permute-done.3 = f32[256,512]{1,0:T(8,128)S(1)} collective-permute-done((f32[256,512]{1,0:T(8,128)}, f32[256,512]{1,0:T(8,128)S(1)}, u32[]{:S(2)}, u32[]{:S(2)}) %collective-permute-start.3) | collective-permute-done | bytes 524320 | tf_op jit(solution)/shard_map/ppermute | solution.py:10
  22.7 8.6 %collective-permute-done.1 = f32[256,512]{1,0:T(8,128)S(1)} collective-permute-done((f32[256,512]{1,0:T(8,128)S(1)}, f32[256,512]{1,0:T(8,128)S(1)}, u32[]{:S(2)}, u32[]{:S(2)}) %collective-permute-start.1) | collective-permute-done | bytes 524320 | tf_op jit(solution)/shard_map/ppermute | solution.py:23
  31.3 14.1 %all-gather.11.cloned.1.call-done = f32[256,1024]{1,0:T(8,128)} async-done(((f32[256,512]{1,0:T(8,128)}), f32[256,1024]{1,0:T(8,128)}) %all-gather.11.cloned.1.call-update) | async-done | bytes 1048592 | tf_op jit(solution)/shard_map/all_gather | solution.py:32
  45.4 5.4 %convert_add_fusion = (f32[256,512]{1,0:T(8,128)}, f32[256,512]{1,0:T(8,128)}) fusion(s32[512]{0:T(512)S(1)} %iota_add_fusion, s32[256]{0:T(256)S(1)} %iota_add_fusion.1, f32[256,1024]{1,0:T(8,128)} %all-gather.11.cloned.1.call-done, s32[]{:T(128)S(6)} %select_n.60, f32[256,512]{1,0:T(8,128)S(1)} %collective-permute-done.2, ...), kind=kOutput, calls=%fused_computation.59 | convolution fusion | flops 1614675968 | bytes 4197380 | tf_op jit(solution)/shard_map/dot_general | solution.py:14
  52.2 8.8 %collective-permute-done.4 = f32[256,512]{1,0:T(8,128)S(1)} collective-permute-done((f32[256,512]{1,0:T(8,128)}, f32[256,512]{1,0:T(8,128)S(1)}, u32[]{:S(2)}, u32[]{:S(2)}) %collective-permute-start.4) | collective-permute-done | bytes 524320 | tf_op jit(solution)/shard_map/ppermute | solution.py:23
  61.1 8.6 %collective-permute-done.5 = f32[256,512]{1,0:T(8,128)S(1)} collective-permute-done((f32[256,512]{1,0:T(8,128)S(1)}, f32[256,512]{1,0:T(8,128)S(1)}, u32[]{:S(2)}, u32[]{:S(2)}) %collective-permute-start.5) | collective-permute-done | bytes 524320 | tf_op jit(solution)/shard_map/ppermute | solution.py:23
  72.2 6.0 %collective-permute-done.6 = f32[256,512]{1,0:T(8,128)S(1)} collective-permute-done((f32[256,512]{1,0:T(8,128)S(1)}, f32[256,512]{1,0:T(8,128)S(1)}, u32[]{:S(2)}, u32[]{:S(2)}) %collective-permute-start.6) | collective-permute-done | bytes 524320 | tf_op jit(solution)/shard_map/ppermute | solution.py:23
  78.3 4.3 %fusion.17 = f32[256,512]{1,0:T(8,128)S(1)} fusion(f32[256,1024]{1,0:T(8,128)} %all-gather.15.cloned.1.call-done, s32[]{:T(128)S(6)} %select_n.60, f32[256,512]{1,0:T(8,128)S(1)} %collective-permute-done.6, f32[256,512]{1,0:T(8,128)S(1)} %collective-permute-done.5, f32[256,512]{1,0:T(8,128)S(1)} %collective-permute-done.4, f32[256,512]{1,0:T(8,128)} %get-tuple-element.11), kind=kOutput, calls=%fused_computation.43 | convolution fusion | flops 1614282752 | bytes 3670020 | tf_op jit(solution)/shard_map/dot_general | solution.py:14
  82.7 8.6 %collective-permute-done.7 = f32[256,512]{1,0:T(8,128)S(1)} collective-permute-done((f32[256,512]{1,0:T(8,128)S(1)}, f32[256,512]{1,0:T(8,128)S(1)}, u32[]{:S(2)}, u32[]{:S(2)}) %collective-permute-start.7) | collective-permute-done | bytes 524320 | tf_op jit(solution)/shard_map/ppermute | solution.py:23
  91.3 8.7 %collective-permute-done.8 = f32[256,512]{1,0:T(8,128)} collective-permute-done((f32[256,512]{1,0:T(8,128)S(1)}, f32[256,512]{1,0:T(8,128)}, u32[]{:S(2)}, u32[]{:S(2)}) %collective-permute-start.8) | collective-permute-done | bytes 524320 | tf_op jit(solution)/shard_map/ppermute | solution.py:23
  100.0 11.3 %collective-permute-done.9 = f32[256,512]{1,0:T(8,128)} collective-permute-done((f32[256,512]{1,0:T(8,128)}, f32[256,512]{1,0:T(8,128)}, u32[]{:S(2)}, u32[]{:S(2)}) %collective-permute-start.9) | collective-permute-done | bytes 524320 | tf_op jit(solution)/shard_map/ppermute | solution.py:23
  111.3 5.2 %fusion.36 = f32[256,512]{1,0:T(8,128)} fusion(f32[256,512]{1,0:T(8,128)S(1)} %copy-done.1, f32[256,1024]{1,0:T(8,128)} %all-gather.13.cloned.1.call-done, s32[]{:T(128)S(6)} %select_n.60, f32[256,512]{1,0:T(8,128)} %collective-permute-done.9, f32[256,512]{1,0:T(8,128)} %collective-permute-done.8, f32[256,512]{1,0:T(8,128)S(1)} %collective-permute-done.7, ...), kind=kOutput, calls=%fused_computation.56 | convolution fusion | flops 1614413824 | bytes 4194308 | tf_op jit(solution)/shard_map/dot_general | solution.py:14
  118.2 35.4 %collective-permute-done.10 = f32[256,1536]{1,0:T(8,128)S(1)} collective-permute-done((f32[256,1536]{1,0:T(8,128)S(1)}, f32[256,1536]{1,0:T(8,128)S(1)}, u32[]{:S(2)}, u32[]{:S(2)}) %collective-permute-start.10) | collective-permute-done | bytes 1572896 | tf_op jit(solution)/shard_map/ppermute | solution.py:10
  153.6 8.1 %broadcast_select_fusion.1 = (f32[256,1536]{1,0:T(8,128)S(1)}, f32[256,1536]{1,0:T(8,128)S(1)}) fusion(f32[256,1536]{1,0:T(8,128)S(1)} %collective-permute-done.10, pred[]{:T(512)S(6)} %eq.10, f32[256,1024]{1,0:T(8,128)} %all-gather.11.cloned.1.call-done, f32[1,1024,1536]{2,1,0:T(8,128)} %all-gather.21.cloned.1.call-done), kind=kOutput, calls=%fused_computation.58 | convolution fusion | flops 4832624640 | bytes 12058625 | tf_op jit(solution)/shard_map/dot_general | solution.py:14
  164.4 6.1 %copy.8 = f32[1,768,1536]{1,2,0:T(8,128)} copy(f32[1,768,1536]{2,1,0:T(8,128)} %param.6) | data formatting | bytes 9437184 | tf_op args[0]
  170.5 6.7 %select_bitcast_fusion.1 = (f32[768,1536]{0,1:T(8,128)}, f32[768,1536]{0,1:T(8,128)}) fusion(f32[1,768,1536]{1,2,0:T(8,128)} %copy.8, pred[]{:T(512)S(6)} %eq.10), kind=kLoop, calls=%fused_computation.4 | loop fusion | flops 2359296 | bytes 14155777 | tf_op jit(solution)/shard_map/jit(_where)/select_n | solution.py:73
  177.3 5.3 %all-gather.19.cloned.1.call-done = f32[2048,512]{1,0:T(8,128)} async-done(((f32[256,512]{1,0:T(8,128)}), f32[2048,512]{1,0:T(8,128)}) %all-gather.19.cloned.1.call-update) | async-done | bytes 4194320 | tf_op jit(solution)/shard_map/all_gather | solution.py:65
  182.5 5.4 %copy.10 = f32[4,2,256,512]{3,1,2,0:T(2,128)S(1)} copy(f32[4,2,256,512]{3,2,1,0:T(8,128)} %bitcast.33) | data formatting | bytes 8388608 | tf_op jit(solution)/shard_map/reshape | solution.py:68
  187.9 3.1 copy.12
  191.0 75.0 %all-gather.17.cloned.1.call-done = f32[1024,3072]{1,0:T(8,128)} async-done(((f32[256,3072]{1,0:T(8,128)}), f32[1024,3072]{1,0:T(8,128)}) %all-gather.17.cloned.1.call-update) | async-done | bytes 12582928 | tf_op jit(solution)/shard_map/all_gather | solution.py:64
  266.0 44.8 %fusion.45 = f32[1024,3072]{1,0:T(8,128)} fusion(f32[1024,1024]{1,0:T(8,128)} %bitcast.34, f32[1024,3072]{1,0:T(8,128)} %all-gather.17.cloned.1.call-done), kind=kOutput, calls=%fused_computation.68 | convolution fusion | flops 38654705664 | bytes 29360128 | tf_op jit(solution)/shard_map/dot_general | solution.py:70
  312.5 64.6 %maximum_add_fusion = f32[768,3072]{0,1:T(8,128)} fusion(f32[768,1536]{0,1:T(8,128)} %get-tuple-element.7, f32[768,1536]{0,1:T(8,128)} %get-tuple-element.6, f32[1024,3072]{1,0:T(8,128)} %fusion.45, f32[1,768,1024]{2,1,0:T(8,128)} %all-gather.23.cloned.1.call-done), kind=kOutput, calls=%fused_computation | convolution fusion | flops 28995747840 | bytes 34603008 | tf_op jit(solution)/shard_map/dot_general | solution.py:14
  377.1 14.8 %copy.11 = f32[1,768,2,1536]{3,2,1,0:T(2,128)} copy(f32[1,768,2,1536]{1,3,2,0:T(8,128)} %bitcast.32) | data formatting | bytes 18874368 | tf_op jit(solution)/shard_map/reshape | solution.py:76
  (39 shorter events, 11.1 us)
Async XLA Ops:
  6.5 38.9 %all-gather.11.cloned.1.call-start = ((), (), s32[]{:S(2)}) async-start(), calls=%async_computation | async-start | bytes 1572864 | tf_op jit(solution)/shard_map/all_gather | solution.py:32
  6.5 15.2 %collective-permute-start.3 = (f32[256,512]{1,0:T(8,128)}, f32[256,512]{1,0:T(8,128)S(1)}, u32[]{:S(2)}, u32[]{:S(2)}) collective-permute-start(f32[256,512]{1,0:T(8,128)} %bitcast.36), channel_id=1, source_target_pairs={{0,8},{8,0},{16,24},{24,16},{1,9},{9,1},{17,25},{25,17},{2,10},{10... | collective-permute-start | bytes 1572872 | tf_op jit(solution)/shard_map/ppermute | solution.py:10
  9.6 13.0 %collective-permute-start = (f32[256,512]{1,0:T(8,128)}, f32[256,512]{1,0:T(8,128)S(1)}, u32[]{:S(2)}, u32[]{:S(2)}) collective-permute-start(f32[256,512]{1,0:T(8,128)} %bitcast.37), channel_id=1, source_target_pairs={{0,2},{2,4},{4,6},{6,0},{1,3},{3,5},{5,7},{7,1},{8,10},{10,12},{12... | collective-permute-start | bytes 1572872 | tf_op jit(solution)/shard_map/ppermute | solution.py:23
  21.7 0.8 copy-start.2
  22.5 49.7 %all-gather.15.cloned.1.call-start = ((), (), s32[]{:S(2)}) async-start(), calls=%async_computation.2 | async-start | bytes 1572864 | tf_op jit(solution)/shard_map/all_gather | solution.py:32
  22.6 8.7 %collective-permute-start.1 = (f32[256,512]{1,0:T(8,128)S(1)}, f32[256,512]{1,0:T(8,128)S(1)}, u32[]{:S(2)}, u32[]{:S(2)}) collective-permute-start(f32[256,512]{1,0:T(8,128)S(1)} %collective-permute-done), channel_id=1, source_target_pairs={{0,2},{2,4},{4,6},{6,0},{1,3},{3,5},{5,7},{7,1},{8,10},{10,12},{12... | collective-permute-start | bytes 1572872 | tf_op jit(solution)/shard_map/ppermute | solution.py:23
  31.3 14.1 %collective-permute-start.2 = (f32[256,512]{1,0:T(8,128)S(1)}, f32[256,512]{1,0:T(8,128)S(1)}, u32[]{:S(2)}, u32[]{:S(2)}) collective-permute-start(f32[256,512]{1,0:T(8,128)S(1)} %collective-permute-done.1), channel_id=1, source_target_pairs={{0,2},{2,4},{4,6},{6,0},{1,3},{3,5},{5,7},{7,1},{8,10},{10,12},{12... | collective-permute-start | bytes 1572872 | tf_op jit(solution)/shard_map/ppermute | solution.py:23
  50.8 49.2 %all-gather.13.cloned.1.call-start = ((), (), s32[]{:S(2)}) async-start(), calls=%async_computation.1 | async-start | bytes 1572864 | tf_op jit(solution)/shard_map/all_gather | solution.py:32
  51.5 102.0 %all-gather.21.cloned.1.call-start = ((), (), s32[]{:S(2)}) async-start(), calls=%async_computation.5 | async-start | bytes 7864320 | tf_op jit(solution)/shard_map/all_gather | solution.py:55
  52.1 59.1 %copy-start.1 = (f32[256,512]{1,0:T(8,128)S(1)}, f32[256,512]{1,0:T(8,128)}, u32[]{:S(2)}) copy-start(f32[256,512]{1,0:T(8,128)} %get-tuple-element.10) | copy-start | bytes 1572868
  52.1 130.4 %all-gather.19.cloned.1.call-start = ((), (), s32[]{:S(2)}) async-start(), calls=%async_computation.4 | async-start | bytes 4718592 | tf_op jit(solution)/shard_map/all_gather | solution.py:65
  52.2 8.9 %collective-permute-start.4 = (f32[256,512]{1,0:T(8,128)}, f32[256,512]{1,0:T(8,128)S(1)}, u32[]{:S(2)}, u32[]{:S(2)}) collective-permute-start(f32[256,512]{1,0:T(8,128)} %get-tuple-element.11), channel_id=1, source_target_pairs={{0,2},{2,4},{4,6},{6,0},{1,3},{3,5},{5,7},{7,1},{8,10},{10,12},{12... | collective-permute-start | bytes 1572872 | tf_op jit(solution)/shard_map/ppermute | solution.py:23
  61.1 8.6 %collective-permute-start.5 = (f32[256,512]{1,0:T(8,128)S(1)}, f32[256,512]{1,0:T(8,128)S(1)}, u32[]{:S(2)}, u32[]{:S(2)}) collective-permute-start(f32[256,512]{1,0:T(8,128)S(1)} %collective-permute-done.4), channel_id=1, source_target_pairs={{0,2},{2,4},{4,6},{6,0},{1,3},{3,5},{5,7},{7,1},{8,10},{10,12},{12... | collective-permute-start | bytes 1572872 | tf_op jit(solution)/shard_map/ppermute | solution.py:23
  69.7 8.6 %collective-permute-start.6 = (f32[256,512]{1,0:T(8,128)S(1)}, f32[256,512]{1,0:T(8,128)S(1)}, u32[]{:S(2)}, u32[]{:S(2)}) collective-permute-start(f32[256,512]{1,0:T(8,128)S(1)} %collective-permute-done.5), channel_id=1, source_target_pairs={{0,2},{2,4},{4,6},{6,0},{1,3},{3,5},{5,7},{7,1},{8,10},{10,12},{12... | collective-permute-start | bytes 1572872 | tf_op jit(solution)/shard_map/ppermute | solution.py:23
  82.6 34.2 %copy-start = (f32[1,256,1536]{2,1,0:T(8,128)S(1)}, f32[1,256,1536]{2,1,0:T(8,128)}, u32[]{:S(2)}) copy-start(f32[1,256,1536]{2,1,0:T(8,128)} %param.8) | copy-start | bytes 4718596
  82.6 8.7 %collective-permute-start.7 = (f32[256,512]{1,0:T(8,128)S(1)}, f32[256,512]{1,0:T(8,128)S(1)}, u32[]{:S(2)}, u32[]{:S(2)}) collective-permute-start(f32[256,512]{1,0:T(8,128)S(1)} %fusion.17), channel_id=1, source_target_pairs={{0,2},{2,4},{4,6},{6,0},{1,3},{3,5},{5,7},{7,1},{8,10},{10,12},{12... | collective-permute-start | bytes 1572872 | tf_op jit(solution)/shard_map/ppermute | solution.py:23
  91.3 8.7 %collective-permute-start.8 = (f32[256,512]{1,0:T(8,128)S(1)}, f32[256,512]{1,0:T(8,128)}, u32[]{:S(2)}, u32[]{:S(2)}) collective-permute-start(f32[256,512]{1,0:T(8,128)S(1)} %collective-permute-done.7), channel_id=1, source_target_pairs={{0,2},{2,4},{4,6},{6,0},{1,3},{3,5},{5,7},{7,1},{8,10},{10,12},{12... | collective-permute-start | bytes 1572872 | tf_op jit(solution)/shard_map/ppermute | solution.py:23
  100.0 11.3 %collective-permute-start.9 = (f32[256,512]{1,0:T(8,128)}, f32[256,512]{1,0:T(8,128)}, u32[]{:S(2)}, u32[]{:S(2)}) collective-permute-start(f32[256,512]{1,0:T(8,128)} %collective-permute-done.8), channel_id=1, source_target_pairs={{0,2},{2,4},{4,6},{6,0},{1,3},{3,5},{5,7},{7,1},{8,10},{10,12},{12... | collective-permute-start | bytes 1572872 | tf_op jit(solution)/shard_map/ppermute | solution.py:23
  116.5 149.5 %all-gather.17.cloned.1.call-start = ((), (), s32[]{:S(2)}) async-start(), calls=%async_computation.3 | async-start | bytes 15728640 | tf_op jit(solution)/shard_map/all_gather | solution.py:64
  116.8 36.8 %collective-permute-start.10 = (f32[256,1536]{1,0:T(8,128)S(1)}, f32[256,1536]{1,0:T(8,128)S(1)}, u32[]{:S(2)}, u32[]{:S(2)}) collective-permute-start(f32[256,1536]{1,0:T(8,128)S(1)} %bitcast.35), channel_id=1, source_target_pairs={{0,8},{8,0},{16,24},{24,16},{1,9},{9,1},{17,25},{25,17},{2,10},{10... | collective-permute-start | bytes 4718600 | tf_op jit(solution)/shard_map/ppermute | solution.py:10
  163.6 148.9 %all-gather.23.cloned.1.call-start = ((), (), s32[]{:S(2)}) async-start(), calls=%async_computation.6 | async-start | bytes 4718592 | tf_op jit(solution)/shard_map/all_gather | solution.py:75
Sparse Core Ops, SparseCore 0:
  22.7 22.6 all-gather.10
  50.9 21.2 all-gather.14
  73.8 21.2 all-gather.12
  96.5 47.6 all-gather.20
  145.9 36.5 all-gather.18
  183.9 82.0 all-gather.16
  267.6 44.8 all-gather.22
